TPU v7x, 128 devices: a whole 4x4x4 slice. The times are simulated.
128 devices in a mesh: seq: 32 (over z, x_lo, y), head: 4 (over x_hi, core).
Axes of the slice: x: 4 (x_hi: 2, x_lo: 2; x = x_hi * 2 + x_lo), y: 4, z: 4, core: 2. Of those that a mesh axis runs over, the one named last changes fastest.
Arguments:
- hidden_in: bfloat16 [12, 2048, 1024], P(None, 'seq'), may hold values from -48 to 48
- lengths: int32 [12], replicated, may hold values from 1 to 2048, as said below
- w_qkv: float32 [1024, 3072], P(('seq', 'head')), may hold values from -0.1875 to 0.1875
- w_attn_out: float32 [1024, 1024], P(('seq', 'head')), may hold values from -0.1875 to 0.1875
- w_in: float32 [1024, 4096], P(('seq', 'head')), may hold values from -0.1875 to 0.1875
- w_down: float32 [4096, 1024], P(('seq', 'head')), may hold values from -0.09375 to 0.09375
- ln_gain: float32 [2, 1024], replicated, may hold values from 0.5 to 1.5
- ln_bias: float32 [2, 1024], replicated, may hold values from -1.5 to 1.5
Outputs:
- hidden_out: bfloat16 [12, 2048, 1024], P(None, 'seq', 'head')
- key_cache: bfloat16 [12, 2048, 1024], P(None, 'seq', 'head')
- value_cache: bfloat16 [12, 2048, 1024], P(None, 'seq', 'head')
Inputs may be any that keep to these rules, and one draw needn't show every extreme that they name: `lengths`: the longest prompt has exactly 2048 positions.
All inputs are finite; a program needn't handle non-finite values.
Results may differ from a plain program's by a relative error of at most 0.014.
Values may be sent and summed in bfloat16 or wider, within the bound.
A program may use at most 192 MiB of HBM per device.

v0:
```python
import jax
import jax.numpy as jnp
from jax import lax
from jax.sharding import PartitionSpec as P

D = 1024
HEADS = 16
HEAD_DIM = 64
EPSILON = 1e-05


def layer_norm(row_values, gain_row, shift_row):
    row_sums, squares = lax.psum(
        (jnp.sum(row_values, axis=1), jnp.sum(row_values * row_values, axis=1)), "head"
    )
    average = (row_sums / D)[:, None]
    spread = (squares / D)[:, None] - average * average
    return (row_values - average) * lax.rsqrt(spread + EPSILON) * gain_row + shift_row


def relayout(qkv_stripe, out_stripe, in_stripe, group_count, seq_count):
    gathered = (
        lax.all_gather(qkv_stripe, "seq", axis=0, tiled=True),
        lax.all_gather(out_stripe, "seq", axis=0, tiled=True),
        lax.all_gather(in_stripe, "seq", axis=0, tiled=True),
    )
    exchanged = (
        lax.all_to_all(gathered[0], "head", split_axis=1, concat_axis=0, tiled=True),
        lax.all_to_all(gathered[1], "head", split_axis=1, concat_axis=0, tiled=True),
        lax.all_to_all(gathered[2], "head", split_axis=1, concat_axis=0, tiled=True),
    )
    result = []
    for piece in exchanged:
        columns = piece.shape[2]
        reordered = piece.reshape(group_count, seq_count, -1, columns).transpose(1, 0, 2, 3)
        result.append(reordered.reshape(-1, columns))
    return tuple(result)


def per_device(hidden_in, lengths, w_qkv, w_attn_out, w_in, w_down, ln_gain, ln_bias):
    group_count = lax.axis_size("head")
    seq_count = lax.axis_size("seq")
    head_group = lax.axis_index("head")
    seq_block = lax.axis_index("seq")
    local_rows = w_qkv.shape[0]
    unit_rows = w_down.shape[0]
    group_width = D // group_count
    heads_here = HEADS // group_count
    prompt_count = hidden_in.shape[0]
    local_span = hidden_in.shape[1]
    qkv_stripe = w_qkv.astype(jnp.bfloat16).reshape(local_rows, 3, group_count, group_width)
    qkv_stripe = qkv_stripe.transpose(0, 2, 1, 3).reshape(local_rows, group_count, 3 * group_width)
    out_stripe = w_attn_out.astype(jnp.bfloat16).reshape(local_rows, group_count, group_width)
    in_stripe = w_in.astype(jnp.bfloat16).reshape(local_rows, seq_count, group_count, unit_rows)
    in_stripe = in_stripe.transpose(0, 2, 1, 3).reshape(
        local_rows, group_count, seq_count * unit_rows
    )
    qkv_weight, out_weight, in_weight = relayout(
        qkv_stripe, out_stripe, in_stripe, group_count, seq_count
    )
    token_rows = hidden_in.reshape(prompt_count * local_span, D)
    projected = jnp.dot(token_rows, qkv_weight, preferred_element_type=jnp.float32).astype(
        jnp.bfloat16
    )
    projected = projected.reshape(prompt_count, local_span, 3, heads_here, HEAD_DIM)
    positions = seq_block * local_span + jnp.arange(local_span, dtype=jnp.int32)
    live_mask = positions[None, :] < lengths[:, None]
    zero_value = jnp.zeros((), jnp.bfloat16)
    queries = projected[:, :, 0]
    keys_here = jnp.where(live_mask[:, :, None, None], projected[:, :, 1], zero_value)
    values_here = jnp.where(live_mask[:, :, None, None], projected[:, :, 2], zero_value)
    keys_all, values_all = (
        lax.all_gather(keys_here, "seq", axis=1, tiled=True),
        lax.all_gather(values_here, "seq", axis=1, tiled=True),
    )
    key_live = jnp.arange(keys_all.shape[1], dtype=jnp.int32)[None, :] < lengths[:, None]
    score_scale = HEAD_DIM ** (-0.5)

    def one_prompt(prompt_items):
        query_rows, key_rows, value_rows, live_keys = prompt_items
        scores = (
            jnp.einsum("qhd,khd->hqk", query_rows, key_rows, preferred_element_type=jnp.float32)
            * score_scale
        )
        scores = jnp.where(live_keys[None, None, :], scores, -jnp.inf)
        row_max = jnp.max(scores, axis=-1, keepdims=True)
        exp_terms = jnp.exp(scores - row_max)
        soft_weights = (exp_terms / jnp.sum(exp_terms, axis=-1, keepdims=True)).astype(jnp.bfloat16)
        head_mix = jnp.einsum(
            "hqk,khd->qhd", soft_weights, value_rows, preferred_element_type=jnp.float32
        )
        return head_mix.astype(jnp.bfloat16)

    attended = lax.map(one_prompt, (queries, keys_all, values_all, key_live))
    attended = attended.reshape(prompt_count * local_span, group_width)
    joined = lax.all_gather(attended, "head", axis=1, tiled=True)
    start = head_group * group_width
    own_columns = lax.dynamic_slice_in_dim(token_rows, start, group_width, 1).astype(jnp.float32)
    gain_first = lax.dynamic_slice_in_dim(ln_gain[0], start, group_width, 0)
    shift_first = lax.dynamic_slice_in_dim(ln_bias[0], start, group_width, 0)
    gain_second = lax.dynamic_slice_in_dim(ln_gain[1], start, group_width, 0)
    shift_second = lax.dynamic_slice_in_dim(ln_bias[1], start, group_width, 0)
    attn_sum = jnp.dot(joined, out_weight, preferred_element_type=jnp.float32) + own_columns
    normed = layer_norm(attn_sum, gain_first, shift_first).astype(jnp.bfloat16)
    normed_all = lax.all_gather(normed, "head", axis=1, tiled=True)
    hidden_units = jax.nn.gelu(
        jnp.dot(normed_all, in_weight, preferred_element_type=jnp.float32), approximate=False
    ).astype(jnp.bfloat16)
    down_weight = lax.all_gather(w_down.astype(jnp.bfloat16), "seq", axis=0, tiled=True)
    partial_terms = jnp.dot(hidden_units, down_weight, preferred_element_type=jnp.float32)
    down_part = lax.psum_scatter(
        partial_terms.astype(jnp.bfloat16), "head", scatter_dimension=1, tiled=True
    ).astype(jnp.float32)
    ffn_sum = down_part + normed.astype(jnp.float32)
    hidden_out = layer_norm(ffn_sum, gain_second, shift_second).astype(jnp.bfloat16)
    hidden_out = hidden_out.reshape(prompt_count, local_span, group_width)
    key_cache = keys_here.reshape(prompt_count, local_span, group_width)
    value_cache = values_here.reshape(prompt_count, local_span, group_width)
    return (hidden_out, key_cache, value_cache)


def solution(mesh):
    in_specs = (
        P(None, "seq", None),
        P(),
        P(("seq", "head"), None),
        P(("seq", "head"), None),
        P(("seq", "head"), None),
        P(("seq", "head"), None),
        P(),
        P(),
    )
    out_specs = (P(None, "seq", "head"), P(None, "seq", "head"), P(None, "seq", "head"))
    return jax.shard_map(
        per_device, mesh=mesh, in_specs=in_specs, out_specs=out_specs, check_vma=False
    )
```

profile of v0, /device:TPU:1, one launch (start us, length us, event | category | flops | bytes accessed | tf_op | source)
XLA Modules:
  0.0 1285.0 jit_solution(5143140646698447728)
XLA Ops:
  8.9 136.6 %all-gather.8.cloned.1.call-done = bf16[256,4,768]{2,0,1:T(8,128)(2,1)} async-done(((bf16[8,4,768]{2,0,1:T(8,128)(2,1)}), bf16[256,4,768]{2,0,1:T(8,128)(2,1)}) %all-gather.8.cloned.1.call-update) | async-done | bytes 1572880 | tf_op jit(solution)/shard_map/all_gather | solution.py:23
  145.4 25.0 %all-to-all-start = ((bf16[256,4,768]{2,0,1:T(8,128)(2,1)}), bf16[256,4,768]{2,0,1:T(8,128)(2,1)S(1)}, u32[]{:S(2)}, u32[]{:S(2)}) async-start(bf16[256,4,768]{2,0,1:T(8,128)(2,1)} %all-gather.8.cloned.1.call-done), calls=%async_computation | async-start | bytes 3145728 | tf_op jit(solution)/shard_map/all_to_all | solution.py:28
  170.7 20.5 %all-to-all-done = bf16[256,4,768]{2,0,1:T(8,128)(2,1)S(1)} async-done(((bf16[256,4,768]{2,0,1:T(8,128)(2,1)}), bf16[256,4,768]{2,0,1:T(8,128)(2,1)S(1)}, u32[]{:S(2)}, u32[]{:S(2)}) %all-to-all-start) | async-done | bytes 1572896 | tf_op jit(solution)/shard_map/all_to_all | solution.py:28
  201.8 275.5 %all-gather.10.cloned.1.call-done = bf16[12,2048,4,64]{3,2,0,1:T(4,128)(2,1)} async-done(((bf16[12,64,4,64]{3,2,0,1:T(4,128)(2,1)}), bf16[12,2048,4,64]{3,2,0,1:T(4,128)(2,1)}) %all-gather.10.cloned.1.call-update) | async-done | bytes 12582928 | tf_op jit(solution)/shard_map/all_gather | solution.py:74
  477.3 35.9 %copy.59 = bf16[12,2048,4,64]{1,3,2,0:T(8,128)(2,1)} copy(bf16[12,2048,4,64]{3,2,0,1:T(4,128)(2,1)} %all-gather.10.cloned.1.call-done) | data formatting | bytes 25165824 | tf_op jit(solution)/shard_map/while | solution.py:94
  513.2 240.0 %all-gather.12.cloned.1.call-done = bf16[12,2048,4,64]{3,2,0,1:T(4,128)(2,1)} async-done(((bf16[12,64,4,64]{3,2,0,1:T(4,128)(2,1)}), bf16[12,2048,4,64]{3,2,0,1:T(4,128)(2,1)}) %all-gather.12.cloned.1.call-update) | async-done | bytes 12582928 | tf_op jit(solution)/shard_map/all_gather | solution.py:73
  753.2 35.9 %copy.60 = bf16[12,2048,4,64]{1,3,2,0:T(8,128)(2,1)} copy(bf16[12,2048,4,64]{3,2,0,1:T(4,128)(2,1)} %all-gather.12.cloned.1.call-done) | data formatting | bytes 25165824 | tf_op jit(solution)/shard_map/while | solution.py:94
  789.1 71.2 %while.10 = (s32[]{:T(128)}, bf16[12,64,4,64]{3,2,1,0:T(4,128)(2,1)S(1)}, bf16[12,2048,4,64]{1,3,2,0:T(8,128)(2,1)}, pred[12,2048]{1,0:T(8,128)(4,1)S(1)}, bf16[...) while((s32[]{:T(128)}, bf16[12,64,4,64]{3,2,1,0:T(4,128)(2,1)S(1)}, ...), condition=%wide.region_3.4_spmd, body=%wide.region_0.3_spmd.sunk | while | flops 137381888 | bytes 6596181 | solution.py:94
  789.1 3.3 fusion.125
  807.0 3.3 fusion.125
  818.8 3.3 fusion.125
  830.7 3.3 fusion.125
  842.5 3.3 fusion.125
  863.6 71.0 %all_gather.28 = bf16[256,4,256]{2,0,1:T(8,128)(2,1)} all-gather(bf16[8,4,256]{2,0,1:T(8,128)(2,1)S(1)} %bitcast.105), channel_id=1, replica_groups=mesh['seq'=32,'head'=4] {'seq'}, dimensions={0}, use_global_device_ids=true | all-gather | bytes 540672 | tf_op jit(solution)/shard_map/all_gather | solution.py:24
  934.6 18.0 %all-to-all-start.1 = ((bf16[256,4,256]{2,0,1:T(8,128)(2,1)}), bf16[256,4,256]{2,0,1:T(8,128)(2,1)S(1)}, u32[]{:S(2)}, u32[]{:S(2)}) async-start(bf16[256,4,256]{2,0,1:T(8,128)(2,1)} %all_gather.28), calls=%async_computation.1 | async-start | bytes 1048576 | tf_op jit(solution)/shard_map/all_to_all | solution.py:29
  952.7 10.4 all-to-all-done.1
  965.3 7.4 all-reduce.1
  973.8 43.7 %all-gather.18.cloned.1.call-done = bf16[256,4,1024]{2,0,1:T(8,128)(2,1)} async-done(((bf16[8,4,1024]{2,0,1:T(8,128)(2,1)}), bf16[256,4,1024]{2,0,1:T(8,128)(2,1)}) %all-gather.18.cloned.1.call-update) | async-done | bytes 2097168 | tf_op jit(solution)/shard_map/all_gather | solution.py:25
  1017.6 54.6 %all_to_all.45 = bf16[256,4,1024]{2,0,1:T(8,128)(2,1)S(1)} all-to-all(bf16[256,4,1024]{2,0,1:T(8,128)(2,1)} %all-gather.18.cloned.1.call-done), channel_id=1, replica_groups=mesh['seq'=32,'head'=4] {'head'}, dimensions={1} | all-to-all | bytes 4194304 | tf_op jit(solution)/shard_map/all_to_all | solution.py:30
  1073.6 100.2 %all-gather.20.cloned.1.call-done = bf16[1024,1024]{1,0:T(8,128)(2,1)} async-done(((bf16[32,1024]{1,0:T(8,128)(2,1)}), bf16[1024,1024]{1,0:T(8,128)(2,1)}) %all-gather.20.cloned.1.call-update) | async-done | bytes 2097168 | tf_op jit(solution)/shard_map/all_gather | solution.py:109
  1173.8 45.7 %all-gather.16.cloned.1.call-done = bf16[768,1024]{1,0:T(8,128)(2,1)} async-done(((bf16[768,256]{1,0:T(8,128)(2,1)}), bf16[768,1024]{1,0:T(8,128)(2,1)}) %all-gather.16.cloned.1.call-update) | async-done | bytes 1572880 | tf_op jit(solution)/shard_map/all_gather | solution.py:105
  1219.6 13.3 %convolution_convert_fusion.1 = bf16[768,1024]{1,0:T(8,128)(2,1)} fusion(bf16[1024,1024]{1,0:T(8,128)(2,1)} %all-gather.20.cloned.1.call-done, bf16[768,1024]{1,0:T(8,128)(2,1)} %all-gather.16.cloned.1.call-done, bf16[1024,1024]{1,0:T(8,128)(2,1)} %bitcast.96), kind=kOutput, calls=%fused_computation.43 | convolution fusion | flops 3273129984 | bytes 7340032 | tf_op jit(solution)/shard_map/dot_general | solution.py:110
  1235.5 31.7 %reduce-scatter.2.cloned.1.call-done = bf16[768,256]{1,0:T(8,128)(2,1)} async-done(((bf16[768,1024]{1,0:T(8,128)(2,1)}), bf16[768,256]{1,0:T(8,128)(2,1)}) %reduce-scatter.2.cloned.1.call-update) | async-done | bytes 393232 | tf_op jit(solution)/shard_map/reduce_scatter | solution.py:111
  1268.6 7.3 all-reduce
  (128 shorter events, 81.1 us)
Async XLA Ops:
  7.2 163.3 %copy-start.8 = (s32[12]{0:T(128)S(1)}, s32[12]{0:T(128)}, u32[]{:S(2)}) copy-start(s32[12]{0:T(128)} %param.11) | copy-start | bytes 148
  7.2 138.3 %all-gather.8.cloned.1.call-start = ((), (), s32[]{:S(2)}) async-start(), calls=%async_computation.4 | async-start | bytes 1622016 | tf_op jit(solution)/shard_map/all_gather | solution.py:23
  145.4 45.8 %all-to-all-start = ((bf16[256,4,768]{2,0,1:T(8,128)(2,1)}), bf16[256,4,768]{2,0,1:T(8,128)(2,1)S(1)}, u32[]{:S(2)}, u32[]{:S(2)}) async-start(bf16[256,4,768]{2,0,1:T(8,128)(2,1)} %all-gather.8.cloned.1.call-done), calls=%async_computation | async-start | bytes 3145728 | tf_op jit(solution)/shard_map/all_to_all | solution.py:28
  170.5 306.8 %all-gather.10.cloned.1.call-start = ((), (), s32[]{:S(2)}) async-start(), calls=%async_computation.5 | async-start | bytes 25952256 | tf_op jit(solution)/shard_map/all_gather | solution.py:74
  197.4 0.9 copy-start
  197.4 4.2 copy-start.2
  200.7 552.5 %all-gather.12.cloned.1.call-start = ((), (), s32[]{:S(2)}) async-start(), calls=%async_computation.6 | async-start | bytes 25952256 | tf_op jit(solution)/shard_map/all_gather | solution.py:73
  201.4 761.7 %all-gather.14.cloned.1.call-start = ((), (), s32[]{:S(2)}) async-start(), calls=%async_computation.7 | async-start | bytes 1966080 | tf_op jit(solution)/shard_map/all_gather | solution.py:96
  789.1 72.5 %copy-start.3 = (f32[8,4096]{1,0:T(8,128)S(1)}, f32[8,4096]{1,0:T(8,128)}, u32[]{:S(2)}) copy-start(f32[8,4096]{1,0:T(8,128)} %param.14) | copy-start | bytes 393220
  789.1 73.8 %copy-start.4 = (f32[32,1024]{1,0:T(8,128)S(1)}, f32[32,1024]{1,0:T(8,128)}, u32[]{:S(2)}) copy-start(f32[32,1024]{1,0:T(8,128)} %param.15) | copy-start | bytes 393220
  860.3 3.3 copy-start.5
  860.3 92.3 %copy-start.6 = (f32[2,1024]{1,0:T(2,128)S(1)}, f32[2,1024]{1,0:T(2,128)}, u32[]{:S(2)}) copy-start(f32[2,1024]{1,0:T(2,128)} %param.16) | copy-start | bytes 24580
  860.3 92.3 %copy-start.7 = (f32[2,1024]{1,0:T(2,128)S(1)}, f32[2,1024]{1,0:T(2,128)}, u32[]{:S(2)}) copy-start(f32[2,1024]{1,0:T(2,128)} %param.17) | copy-start | bytes 24580
  861.6 156.0 %all-gather.18.cloned.1.call-start = ((), (), s32[]{:S(2)}) async-start(), calls=%async_computation.9 | async-start | bytes 2162688 | tf_op jit(solution)/shard_map/all_gather | solution.py:25
  862.8 311.0 %all-gather.20.cloned.1.call-start = ((), (), s32[]{:S(2)}) async-start(), calls=%async_computation.10 | async-start | bytes 2162688 | tf_op jit(solution)/shard_map/all_gather | solution.py:109
  934.6 28.5 %all-to-all-start.1 = ((bf16[256,4,256]{2,0,1:T(8,128)(2,1)}), bf16[256,4,256]{2,0,1:T(8,128)(2,1)S(1)}, u32[]{:S(2)}, u32[]{:S(2)}) async-start(bf16[256,4,256]{2,0,1:T(8,128)(2,1)} %all_gather.28), calls=%async_computation.1 | async-start | bytes 1048576 | tf_op jit(solution)/shard_map/all_to_all | solution.py:29
  952.6 267.0 %all-gather.16.cloned.1.call-start = ((), (), s32[]{:S(2)}) async-start(), calls=%async_computation.8 | async-start | bytes 1966080 | tf_op jit(solution)/shard_map/all_gather | solution.py:105
  973.8 293.4 %reduce-scatter.2.cloned.1.call-start = ((), (), s32[]{:S(2)}) async-start(), calls=%async_computation.11 | async-start | bytes 1966080 | tf_op jit(solution)/shard_map/reduce_scatter | solution.py:111
  1219.6 13.3 %copy-start.1 = (bf16[12,64,1,4,64]{4,3,2,1,0:T(4,128)(2,1)S(1)}, bf16[12,64,1,4,64]{4,3,2,1,0:T(4,128)(2,1)}, u32[]{:S(2)}) copy-start(bf16[12,64,1,4,64]{4,3,2,1,0:T(4,128)(2,1)} %copy-done) | copy-start | bytes 1179652
Sparse Core Ops, SparseCore 0:
  10.2 135.1 all-gather.7
  200.8 276.4 all-gather.9
  478.9 274.2 all-gather.11
  861.7 21.3 all-gather.13
  885.2 132.3 all-gather.17
  1019.7 154.1 all-gather.19
  1176.1 43.4 all-gather.15
  1233.0 34.1 reduce-scatter.1
where the time goes:
time: 1290 us
  waiting for transfers between devices  905 us (70%)
  blocking collectives  140 us (11%)
  matrix products  86.7 us (7%)
  local copies, waits for them, and re-layouts  84.7 us (7%)
  starting transfers between devices  43.3 us (3%)
  between operations  14.4 us (1%)
    all_gather x1, waiting for transfers between devices, per_device(): lax.all_gather(values_here, 'seq', axis=1, tiled=True)  275 us
    all_gather x1, waiting for transfers between devices, per_device(): lax.all_gather(keys_here, 'seq', axis=1, tiled=True)  240 us
    all_gather x1, waiting for transfers between devices, relayout(): lax.all_gather(qkv_stripe, 'seq', axis=0, tiled=True)  137 us
    all_gather x1, waiting for transfers between devices, per_device(): lax.all_gather(w_down.astype(jnp.bfloat16), 'seq', axis=0, tiled=True)  100 us
    while x2, local copies, waits for them, and re-layouts, per_device(): attended = lax.map(one_prompt, (queries, keys_all, values_all, key_live))  71.8 us
    all_gather x1, blocking collectives, relayout(): lax.all_gather(out_stripe, 'seq', axis=0, tiled=True)  71 us
    all_to_all x1, blocking collectives, relayout(): lax.all_to_all(gathered[2], 'head', split_axis=1, concat_axis=0, tiled=True)  54.6 us
    all_gather x1, waiting for transfers between devices, per_device(): normed_all = lax.all_gather(normed, 'head', axis=1, tiled=True)  45.7 us
  transfers between devices with their start and end apart: 10, of which 9 were waited for; matrix products, arithmetic and copies ran while one was open for 4% of the time, Pallas kernels for 0%

commit v1 on v0

--- a/solution.py
+++ b/solution.py
@@ -20,7 +20,9 @@
 
 def relayout(qkv_stripe, out_stripe, in_stripe, group_count, seq_count):
     gathered = (
-        lax.all_gather(qkv_stripe, "seq", axis=0, tiled=True),
+        jnp.concatenate(
+            lax.all_to_all(jnp.stack([qkv_stripe] * lax.axis_size("seq")), "seq", 0, 0), axis=0
+        ),
         lax.all_gather(out_stripe, "seq", axis=0, tiled=True),
         lax.all_gather(in_stripe, "seq", axis=0, tiled=True),
     )

time: 1290 us -> 1160 us (0.90)
  waiting for transfers between devices: 905 us -> 765 us
  blocking collectives: 140 us -> 171 us
  starting transfers between devices: 43.3 us -> 25 us
    all_gather x1 -> x0, waiting for transfers between devices: 137 us -> none  [relayout(): lax.all_gather(qkv_stripe, 'seq', axis=0, tiled=True)]
    all_to_all x0 -> x1, blocking collectives: none -> 30.7 us  [relayout(): lax.all_to_all(jnp.stack([qkv_stripe] * lax.axis_size('seq')), 'seq', 0, 0)]
    all_to_all x1, starting transfers between devices: 25 us -> 6.6 us  [relayout(): lax.all_to_all(gathered[0], 'head', split_axis=1, concat_axis=0, tiled=True)]
  transfers between devices with their start and end apart: 10 -> 9, of which waited for: 9 -> 8; matrix products, arithmetic and copies ran while one was open for 4% -> 4% of each run, Pallas kernels for 0% -> 0%
where the time goes in v1:
time: 1160 us
  waiting for transfers between devices  765 us (66%)
  blocking collectives  171 us (15%)
  matrix products  86.5 us (7%)
  local copies, waits for them, and re-layouts  85.5 us (7%)
  starting transfers between devices  25 us (2%)
  between operations  14.4 us (1%)
    all_gather x1, waiting for transfers between devices, per_device(): lax.all_gather(values_here, 'seq', axis=1, tiled=True)  273 us
    all_gather x1, waiting for transfers between devices, per_device(): lax.all_gather(keys_here, 'seq', axis=1, tiled=True)  240 us
    all_gather x1, waiting for transfers between devices, per_device(): lax.all_gather(w_down.astype(jnp.bfloat16), 'seq', axis=0, tiled=True)  100 us
    while x2, local copies, waits for them, and re-layouts, per_device(): attended = lax.map(one_prompt, (queries, keys_all, values_all, key_live))  71.7 us
    all_gather x1, blocking collectives, relayout(): lax.all_gather(out_stripe, 'seq', axis=0, tiled=True)  70.9 us
    all_to_all x1, blocking collectives, relayout(): lax.all_to_all(gathered[2], 'head', split_axis=1, concat_axis=0, tiled=True)  54.4 us
    all_gather x1, waiting for transfers between devices, per_device(): normed_all = lax.all_gather(normed, 'head', axis=1, tiled=True)  45.6 us
    all_gather x1, waiting for transfers between devices, relayout(): lax.all_gather(in_stripe, 'seq', axis=0, tiled=True)  43.8 us
  transfers between devices with their start and end apart: 9, of which 8 were waited for; matrix products, arithmetic and copies ran while one was open for 4% of the time, Pallas kernels for 0%

profile of v1, /device:TPU:1, one launch (start us, length us, event | category | flops | bytes accessed | tf_op | source)
XLA Modules:
  0.0 1158.1 jit_solution(3501247636033793067)
XLA Ops:
  8.4 30.7 %all_to_all.50 = bf16[32,8,4,768]{3,1,2,0:T(8,128)(2,1)S(1)} all-to-all(bf16[32,8,4,768]{3,1,2,0:T(8,128)(2,1)S(1)} %stack.3), channel_id=1, replica_groups=mesh['seq'=32,'head'=4] {'seq'}, dimensions={0} | all-to-all | bytes 3145728 | tf_op jit(solution)/shard_map/all_to_all | solution.py:24
  40.4 6.6 all-to-all-start.1
  47.2 20.5 %all-to-all-done.1 = bf16[256,4,768]{2,0,1:T(8,128)(2,1)S(1)} async-done(((bf16[256,4,768]{2,0,1:T(8,128)(2,1)}), bf16[256,4,768]{2,0,1:T(8,128)(2,1)S(1)}, u32[]{:S(2)}, u32[]{:S(2)}) %all-to-all-start.1) | async-done | bytes 1572896 | tf_op jit(solution)/shard_map/all_to_all | solution.py:30
  78.3 272.6 %all-gather.7.cloned.1.call-done = bf16[12,2048,4,64]{3,2,0,1:T(4,128)(2,1)} async-done(((bf16[12,64,4,64]{3,2,0,1:T(4,128)(2,1)}), bf16[12,2048,4,64]{3,2,0,1:T(4,128)(2,1)}) %all-gather.7.cloned.1.call-update) | async-done | bytes 12582928 | tf_op jit(solution)/shard_map/all_gather | solution.py:76
  350.9 35.9 %copy.61 = bf16[12,2048,4,64]{1,3,2,0:T(8,128)(2,1)} copy(bf16[12,2048,4,64]{3,2,0,1:T(4,128)(2,1)} %all-gather.7.cloned.1.call-done) | data formatting | bytes 25165824 | tf_op jit(solution)/shard_map/while | solution.py:96
  386.8 240.0 %all-gather.9.cloned.1.call-done = bf16[12,2048,4,64]{3,2,0,1:T(4,128)(2,1)} async-done(((bf16[12,64,4,64]{3,2,0,1:T(4,128)(2,1)}), bf16[12,2048,4,64]{3,2,0,1:T(4,128)(2,1)}) %all-gather.9.cloned.1.call-update) | async-done | bytes 12582928 | tf_op jit(solution)/shard_map/all_gather | solution.py:75
  626.8 35.8 %copy.62 = bf16[12,2048,4,64]{1,3,2,0:T(8,128)(2,1)} copy(bf16[12,2048,4,64]{3,2,0,1:T(4,128)(2,1)} %all-gather.9.cloned.1.call-done) | data formatting | bytes 25165824 | tf_op jit(solution)/shard_map/while | solution.py:96
  662.6 71.0 %while.10 = (s32[]{:T(128)}, bf16[12,64,4,64]{3,2,1,0:T(4,128)(2,1)S(1)}, bf16[12,2048,4,64]{1,3,2,0:T(8,128)(2,1)}, pred[12,2048]{1,0:T(8,128)(4,1)S(1)}, bf16[...) while((s32[]{:T(128)}, bf16[12,64,4,64]{3,2,1,0:T(4,128)(2,1)S(1)}, ...), condition=%wide.region_3.4_spmd, body=%wide.region_0.3_spmd.sunk | while | flops 137381888 | bytes 6596181 | solution.py:96
  662.7 3.3 fusion.125
  668.7 3.3 fusion.125
  674.6 3.3 fusion.125
  680.5 3.3 fusion.125
  686.4 3.3 fusion.125
  736.9 70.9 %all_gather.24 = bf16[256,4,256]{2,0,1:T(8,128)(2,1)} all-gather(bf16[8,4,256]{2,0,1:T(8,128)(2,1)S(1)} %bitcast.108), channel_id=1, replica_groups=mesh['seq'=32,'head'=4] {'seq'}, dimensions={0}, use_global_device_ids=true | all-gather | bytes 540672 | tf_op jit(solution)/shard_map/all_gather | solution.py:26
  807.8 18.2 %all-to-all-start.2 = ((bf16[256,4,256]{2,0,1:T(8,128)(2,1)}), bf16[256,4,256]{2,0,1:T(8,128)(2,1)S(1)}, u32[]{:S(2)}, u32[]{:S(2)}) async-start(bf16[256,4,256]{2,0,1:T(8,128)(2,1)} %all_gather.24), calls=%async_computation.2 | async-start | bytes 1048576 | tf_op jit(solution)/shard_map/all_to_all | solution.py:31
  826.1 10.3 all-to-all-done.2
  838.6 7.5 all-reduce.1
  847.2 43.8 %all-gather.15.cloned.1.call-done = bf16[256,4,1024]{2,0,1:T(8,128)(2,1)} async-done(((bf16[8,4,1024]{2,0,1:T(8,128)(2,1)}), bf16[256,4,1024]{2,0,1:T(8,128)(2,1)}) %all-gather.15.cloned.1.call-update) | async-done | bytes 2097168 | tf_op jit(solution)/shard_map/all_gather | solution.py:27
  891.0 54.4 %all_to_all.51 = bf16[256,4,1024]{2,0,1:T(8,128)(2,1)S(1)} all-to-all(bf16[256,4,1024]{2,0,1:T(8,128)(2,1)} %all-gather.15.cloned.1.call-done), channel_id=1, replica_groups=mesh['seq'=32,'head'=4] {'head'}, dimensions={1} | all-to-all | bytes 4194304 | tf_op jit(solution)/shard_map/all_to_all | solution.py:32
  946.9 100.1 %all-gather.17.cloned.1.call-done = bf16[1024,1024]{1,0:T(8,128)(2,1)} async-done(((bf16[32,1024]{1,0:T(8,128)(2,1)}), bf16[1024,1024]{1,0:T(8,128)(2,1)}) %all-gather.17.cloned.1.call-update) | async-done | bytes 2097168 | tf_op jit(solution)/shard_map/all_gather | solution.py:111
  1047.1 45.6 %all-gather.13.cloned.1.call-done = bf16[768,1024]{1,0:T(8,128)(2,1)} async-done(((bf16[768,256]{1,0:T(8,128)(2,1)}), bf16[768,1024]{1,0:T(8,128)(2,1)}) %all-gather.13.cloned.1.call-update) | async-done | bytes 1572880 | tf_op jit(solution)/shard_map/all_gather | solution.py:107
  1092.6 13.3 %convolution_convert_fusion.1 = bf16[768,1024]{1,0:T(8,128)(2,1)} fusion(bf16[1024,1024]{1,0:T(8,128)(2,1)} %all-gather.17.cloned.1.call-done, bf16[768,1024]{1,0:T(8,128)(2,1)} %all-gather.13.cloned.1.call-done, bf16[1024,1024]{1,0:T(8,128)(2,1)} %bitcast.99), kind=kOutput, calls=%fused_computation.43 | convolution fusion | flops 3273129984 | bytes 7340032 | tf_op jit(solution)/shard_map/dot_general | solution.py:112
  1108.6 31.6 %reduce-scatter.2.cloned.1.call-done = bf16[768,256]{1,0:T(8,128)(2,1)} async-done(((bf16[768,1024]{1,0:T(8,128)(2,1)}), bf16[768,256]{1,0:T(8,128)(2,1)}) %reduce-scatter.2.cloned.1.call-update) | async-done | bytes 393232 | tf_op jit(solution)/shard_map/reduce_scatter | solution.py:113
  1141.7 7.3 all-reduce
  (128 shorter events, 81.7 us)
Async XLA Ops:
  39.1 7.9 copy-start.8
  40.4 27.3 %all-to-all-start.1 = ((bf16[256,4,768]{2,0,1:T(8,128)(2,1)}), bf16[256,4,768]{2,0,1:T(8,128)(2,1)S(1)}, u32[]{:S(2)}, u32[]{:S(2)}) async-start(bf16[256,4,768]{2,0,1:T(8,128)(2,1)} %bitcast.85), calls=%async_computation.1 | async-start | bytes 3145728 | tf_op jit(solution)/shard_map/all_to_all | solution.py:30
  47.0 303.9 %all-gather.7.cloned.1.call-start = ((), (), s32[]{:S(2)}) async-start(), calls=%async_computation.5 | async-start | bytes 25952256 | tf_op jit(solution)/shard_map/all_gather | solution.py:76
  73.8 0.9 copy-start
  73.8 4.2 copy-start.2
  77.2 549.7 %all-gather.9.cloned.1.call-start = ((), (), s32[]{:S(2)}) async-start(), calls=%async_computation.6 | async-start | bytes 25952256 | tf_op jit(solution)/shard_map/all_gather | solution.py:75
  77.9 758.5 %all-gather.11.cloned.1.call-start = ((), (), s32[]{:S(2)}) async-start(), calls=%async_computation.7 | async-start | bytes 1966080 | tf_op jit(solution)/shard_map/all_gather | solution.py:98
  662.6 72.4 %copy-start.3 = (f32[8,4096]{1,0:T(8,128)S(1)}, f32[8,4096]{1,0:T(8,128)}, u32[]{:S(2)}) copy-start(f32[8,4096]{1,0:T(8,128)} %param.14) | copy-start | bytes 393220
  662.6 73.6 %copy-start.4 = (f32[32,1024]{1,0:T(8,128)S(1)}, f32[32,1024]{1,0:T(8,128)}, u32[]{:S(2)}) copy-start(f32[32,1024]{1,0:T(8,128)} %param.15) | copy-start | bytes 393220
  733.6 3.3 copy-start.5
  733.6 92.3 %copy-start.6 = (f32[2,1024]{1,0:T(2,128)S(1)}, f32[2,1024]{1,0:T(2,128)}, u32[]{:S(2)}) copy-start(f32[2,1024]{1,0:T(2,128)} %param.16) | copy-start | bytes 24580
  733.7 92.4 %copy-start.7 = (f32[2,1024]{1,0:T(2,128)S(1)}, f32[2,1024]{1,0:T(2,128)}, u32[]{:S(2)}) copy-start(f32[2,1024]{1,0:T(2,128)} %param.17) | copy-start | bytes 24580
  734.9 156.1 %all-gather.15.cloned.1.call-start = ((), (), s32[]{:S(2)}) async-start(), calls=%async_computation.9 | async-start | bytes 2162688 | tf_op jit(solution)/shard_map/all_gather | solution.py:27
  736.2 310.9 %all-gather.17.cloned.1.call-start = ((), (), s32[]{:S(2)}) async-start(), calls=%async_computation.10 | async-start | bytes 2162688 | tf_op jit(solution)/shard_map/all_gather | solution.py:111
  807.8 28.5 %all-to-all-start.2 = ((bf16[256,4,256]{2,0,1:T(8,128)(2,1)}), bf16[256,4,256]{2,0,1:T(8,128)(2,1)S(1)}, u32[]{:S(2)}, u32[]{:S(2)}) async-start(bf16[256,4,256]{2,0,1:T(8,128)(2,1)} %all_gather.24), calls=%async_computation.2 | async-start | bytes 1048576 | tf_op jit(solution)/shard_map/all_to_all | solution.py:31
  826.0 266.7 %all-gather.13.cloned.1.call-start = ((), (), s32[]{:S(2)}) async-start(), calls=%async_computation.8 | async-start | bytes 1966080 | tf_op jit(solution)/shard_map/all_gather | solution.py:107
  847.1 293.1 %reduce-scatter.2.cloned.1.call-start = ((), (), s32[]{:S(2)}) async-start(), calls=%async_computation.11 | async-start | bytes 1966080 | tf_op jit(solution)/shard_map/reduce_scatter | solution.py:113
  1092.6 13.4 %copy-start.1 = (bf16[12,64,1,4,64]{4,3,2,1,0:T(4,128)(2,1)S(1)}, bf16[12,64,1,4,64]{4,3,2,1,0:T(4,128)(2,1)}, u32[]{:S(2)}) copy-start(bf16[12,64,1,4,64]{4,3,2,1,0:T(4,128)(2,1)} %copy-done) | copy-start | bytes 1179652
Sparse Core Ops, SparseCore 0:
  77.3 273.5 all-gather.6
  352.5 274.2 all-gather.8
  735.0 21.3 all-gather.10
  758.5 132.4 all-gather.14
  893.1 153.9 all-gather.16
  1049.1 43.4 all-gather.12
  1106.1 34.0 reduce-scatter.1
